TPU v7x, 128 devices: a whole 4x4x4 slice. The times are simulated.
128 devices in a mesh: dp: 8 (over z_lo, y), sp: 16 (over x, z_hi, core).
Axes of the slice: x: 4, y: 4, z: 4 (z_hi: 2, z_lo: 2; z = z_hi * 2 + z_lo), core: 2. Of those that a mesh axis runs over, the one named last changes fastest.
Arguments:
- feats: bfloat16 [8, 32, 256, 128], P('dp', None, 'sp'), may hold values from -62 to 62
- conv_w: bfloat16 [1152, 256], replicated, may hold values from -0.1875 to 0.1875
- group_norm_gain: float32 [256], replicated, may hold values from 0.5 to 1.5
- group_norm_bias: float32 [256], replicated, may hold values from -3 to 3
- emb_w: bfloat16 [256, 3072], replicated, may hold values from -0.375 to 0.375
- time_w: bfloat16 [256, 9216], replicated, may hold values from -0.375 to 0.375
- up_w: bfloat16 [3072, 6144], P(None, 'sp'), may hold values from -0.109375 to 0.109375
- down_w: bfloat16 [6144, 3072], P('sp'), may hold values from -0.078125 to 0.078125
- steps: int32 [8], P('dp'), may hold values from 0 to 999
- cotangent: bfloat16 [8, 2048, 3072], P('dp', 'sp'), may hold values from -28 to 28
Outputs:
- grad_conv: float32 [1152, 256], replicated
- grad_up: float32 [3072, 6144], P('dp', 'sp')
- grad_down: float32 [6144, 3072], P('sp', 'dp')
All inputs are finite; a program needn't handle non-finite values.
Results may differ from a plain program's by a relative error of at most 0.012.
Values may be sent and summed in bfloat16 or wider, within the bound.
A program may use at most 192 MiB of HBM per device.

v0:
```python
import math
import jax
import jax.numpy as jnp
from jax import lax
from jax.sharding import Mesh
from jax.sharding import PartitionSpec as P

NORM_GROUPS = 32
SP = ("sp_0", "sp_1", "sp_2")
DP_SP = ("dp", "sp_0", "sp_1", "sp_2")


def from_behind(array, axis, by):
    length = lax.axis_size(axis)
    pairs = [(i, i + by) for i in range(length) if 0 <= i + by < length]
    return lax.ppermute(array, axis, pairs)


def copy_for_each(array, axis):
    length = lax.axis_size(axis)
    return lax.all_to_all(
        jnp.broadcast_to(array[None], (length, *array.shape)), axis, 0, 0, tiled=True
    )


def over_copies(array, axis):
    return copy_for_each(array, axis).sum(axis=0)


def in_one(arrays, axis):
    ends = [0]
    for a in arrays:
        ends.append(ends[-1] + a.size)
    subtotal = over_copies(jnp.concatenate([a.ravel() for a in arrays]), axis)
    return tuple((subtotal[b:e].reshape(a.shape) for a, b, e in zip(arrays, ends, ends[1:])))


def in_blocks(array, dim, length):
    before, after = (array.shape[:dim], array.shape[dim + 1 :])
    return jnp.moveaxis(array.reshape(*before, length, -1, *after), dim, 0)


def sum_by_chip(array, chips, core, dim):
    sizes = (lax.axis_size(chips), lax.axis_size(core))
    parts = in_blocks(array, dim, sizes[0] * sizes[1])
    inside = parts.shape[1:]
    parts = parts.reshape(*sizes, *inside).swapaxes(0, 1).reshape(-1, *inside)
    parts = lax.psum_scatter(parts, core, scatter_dimension=0, tiled=True)
    return lax.psum_scatter(parts, chips, scatter_dimension=0, tiled=True)[0]


def sum_packed(arrays, axis, dims):
    length = lax.axis_size(axis)
    parts = [in_blocks(a, dim, length) for a, dim in zip(arrays, dims)]
    lines = jnp.concatenate([b.reshape(length, -1) for b in parts], axis=1)
    rows = max(16, -(-lines.shape[1] // 1024) * 8)
    lines = jnp.pad(lines, ((0, 0), (0, rows * 128 - lines.shape[1]))).reshape(-1, 128)
    ravelled, at, finished = (lax.psum_scatter(lines, axis, tiled=True).reshape(-1), 0, [])
    for b in parts:
        part = b[0]
        finished.append(ravelled[at : at + part.size].reshape(part.shape))
        at += part.size
    return tuple(finished)


def gelu_pair(u):
    coef = math.sqrt(2.0 / math.pi)
    inner = coef * (u + 0.044715 * u * u * u)
    tangent = jnp.tanh(inner)
    value = 0.5 * u * (1.0 + tangent)
    slope = 0.5 * (1.0 + tangent) + 0.5 * u * (1.0 - tangent * tangent) * coef * (
        1.0 + 3.0 * 0.044715 * u * u
    )
    return (value, slope)


def silu_pair(value):
    sigma = jax.nn.sigmoid(value)
    return (value * sigma, sigma * (1.0 + value * (1.0 - sigma)))


def modulation(step_value, time_w):
    half = time_w.shape[0] // 2
    freqs = jnp.exp(-math.log(10000.0) * jnp.arange(half, dtype=jnp.float32) / half)
    angle = step_value.astype(jnp.float32) * freqs
    embed = jnp.concatenate([jnp.cos(angle), jnp.sin(angle)])
    mixed = jnp.dot(
        jax.nn.silu(embed).astype(jnp.bfloat16)[None, :], time_w, preferred_element_type=jnp.float32
    )[0]
    width = time_w.shape[1] // 3
    return (mixed[:width], mixed[width : 2 * width], mixed[2 * width :])


def make_patches(padded, rows, cols):
    pieces = []
    for row_tap in range(3):
        for col_tap in range(3):
            pieces.append(
                padded[row_tap : row_tap + 2 * rows : 2, col_tap : col_tap + 2 * cols : 2, :]
            )
    stacked = jnp.concatenate(pieces, axis=-1)
    return stacked.reshape(rows * cols, stacked.shape[-1])


def group_totals(first, second, groups):
    tokens, width = first.shape
    first_g = first.reshape(tokens, groups, width // groups)
    second_g = second.reshape(tokens, groups, width // groups)
    return (jnp.sum(first_g, axis=(0, 2)), jnp.sum(second_g, axis=(0, 2)))


def broadcast_groups(values, width):
    return jnp.repeat(values, width // values.shape[0])


def contract(left, right, left_dim, right_dim):
    return lax.dot_general(
        left, right, (((left_dim,), (right_dim,)), ((), ())), preferred_element_type=jnp.float32
    )


def on_device(
    feats, conv_w, group_norm_gain, group_norm_bias, emb_w, time_w, up_w, down_w, steps, cotangent
):
    devices_sp = lax.axis_size(SP)
    image = feats[0]
    rows_in, cols_in, _ = image.shape
    rows = rows_in // 2
    cols = cols_in // 2
    seq_rows = rows // devices_sp
    channel_count = conv_w.shape[1]
    rim = from_behind(image[:, cols_in - 1, :], SP, 1)
    widened = jnp.concatenate([rim[:, None, :], image], axis=1)
    padded = jnp.pad(widened, ((1, 0), (0, 0), (0, 0)))
    patches = make_patches(padded, rows, cols)
    normed_value = jnp.dot(patches, conv_w, preferred_element_type=jnp.float32)
    first, second = group_totals(normed_value, normed_value * normed_value, NORM_GROUPS)
    first, second = in_one((first, second), SP)
    group_count = normed_value.shape[0] * devices_sp * (channel_count // NORM_GROUPS)
    group_mean = first / group_count
    rstd = lax.rsqrt(second / group_count - group_mean * group_mean + 1e-05)
    channel_rstd = broadcast_groups(rstd, channel_count)
    centered_input = (normed_value - broadcast_groups(group_mean, channel_count)) * channel_rstd
    preactivation = centered_input * group_norm_gain + group_norm_bias
    act_val, silu_slope = silu_pair(preactivation)
    act_b = act_val.astype(jnp.bfloat16)
    shift, scale, gate = modulation(steps[0], time_w)
    cot_seq = cotangent[0]
    width = emb_w.shape[1]
    all_cot = lax.all_gather(cot_seq, SP, axis=0, tiled=True)
    all_act = lax.all_gather(act_b.reshape(rows, cols, channel_count), SP, axis=1, tiled=True)
    all_act = all_act.reshape(rows * cols * devices_sp, channel_count)
    emb_f = emb_w.astype(jnp.float32)
    emb_mean = jnp.mean(emb_f, axis=1, keepdims=True)
    gram = contract(emb_w, emb_w, 1, 1) - width * emb_mean * emb_mean.T
    gram_hi = gram.astype(jnp.bfloat16)
    gram_lo = (gram - gram_hi.astype(jnp.float32)).astype(jnp.bfloat16)
    emb_c = emb_f - emb_mean
    mixer = jnp.dot(
        (emb_c * (1.0 + scale)).astype(jnp.bfloat16), up_w, preferred_element_type=jnp.float32
    ).astype(jnp.bfloat16)
    shift_hi = shift.astype(jnp.bfloat16)
    shift_lo = (shift - shift_hi.astype(jnp.float32)).astype(jnp.bfloat16)
    offset = jnp.dot(jnp.stack([shift_hi, shift_lo]), up_w, preferred_element_type=jnp.float32).sum(
        axis=0
    )
    act_gram = jnp.dot(all_act, gram_hi, preferred_element_type=jnp.float32) + jnp.dot(
        all_act, gram_lo, preferred_element_type=jnp.float32
    )
    token_var = jnp.sum(all_act.astype(jnp.float32) * act_gram, axis=-1, keepdims=True) / width
    token_rstd = lax.rsqrt(token_var + 1e-06)
    moved = token_rstd * jnp.dot(all_act, mixer, preferred_element_type=jnp.float32)
    gelu_val, gelu_slope = gelu_pair(moved + offset)
    hid = gelu_val.astype(jnp.bfloat16)
    dhid = contract(all_cot, (down_w.astype(jnp.float32) * gate).astype(jnp.bfloat16), 1, 1)
    dupper = dhid * gelu_slope
    dupper_sum = jnp.sum(dupper, axis=0)
    dupper_r = (dupper * token_rstd).astype(jnp.bfloat16)
    cross = jnp.sum(dupper_r.astype(jnp.float32) * moved, axis=-1, keepdims=True)
    part = contract(dupper_r, mixer, 1, 1) - cross * token_rstd * act_gram / width
    dact = sum_by_chip(part.astype(jnp.bfloat16), ("sp_0", "sp_1"), "sp_2", 0).astype(jnp.float32)
    dact = dact + contract(cot_seq, emb_w, 1, 1)
    pair = contract(all_act, dupper_r, 0, 0).astype(jnp.bfloat16)
    grad_down_local = contract(hid, all_cot, 0, 0) * gate
    (grad_down,) = sum_packed((grad_down_local.astype(jnp.bfloat16),), "dp", (1,))
    grad_down = grad_down.astype(jnp.float32)
    all_pair = lax.all_gather(pair, "dp", axis=0, tiled=True)
    side = lax.all_gather(jnp.concatenate([1.0 + scale, shift, dupper_sum]), "dp", axis=0)
    here = lax.axis_index("dp")
    block = width // lax.axis_size("dp")
    emb_here = lax.dynamic_slice_in_dim(emb_c, here * block, block, 1)
    scale_here = lax.dynamic_slice_in_dim(side[:, :width], here * block, block, 1)
    shift_here = lax.dynamic_slice_in_dim(side[:, width : 2 * width], here * block, block, 1)
    left = (emb_here[None] * scale_here[:, None, :]).astype(jnp.bfloat16)
    grad_up = contract(left.reshape(-1, block), all_pair, 0, 0) + lax.dot_general(
        shift_here, side[:, 2 * width :], (((0,), (0,)), ((), ())), precision=lax.Precision.HIGHEST
    )
    back_tiles = lax.all_to_all(
        dact.reshape(seq_rows, cols * devices_sp, channel_count).astype(jnp.bfloat16),
        SP,
        split_axis=1,
        concat_axis=0,
        tiled=True,
    ).astype(jnp.float32)
    dact_tile = back_tiles.reshape(rows * cols, channel_count)
    input_gradient = dact_tile * silu_slope * group_norm_gain
    backward_first, backward_second = group_totals(
        input_gradient, input_gradient * centered_input, NORM_GROUPS
    )
    backward_first, backward_second = in_one((backward_first, backward_second), SP)
    normed_gradient = (
        channel_rstd
        * (
            input_gradient
            - broadcast_groups(backward_first / group_count, channel_count)
            - centered_input * broadcast_groups(backward_second / group_count, channel_count)
        )
    ).astype(jnp.bfloat16)
    conv_local = contract(patches, normed_gradient, 0, 0)
    grad_conv = lax.psum(conv_local, DP_SP)
    return (grad_conv, grad_up, grad_down)


def solution(mesh):
    finer = Mesh(mesh.devices.reshape(mesh.shape["dp"], 4, 2, 2), ("dp", "sp_0", "sp_1", "sp_2"))
    in_specs = (
        P("dp", None, SP, None),
        P(),
        P(),
        P(),
        P(),
        P(),
        P(None, SP),
        P(SP, None),
        P("dp"),
        P("dp", SP, None),
    )
    out_specs = (P(), P("dp", SP), P(SP, "dp"))
    return jax.shard_map(
        on_device, mesh=finer, in_specs=in_specs, out_specs=out_specs, check_vma=False
    )
```

profile of v0, /device:TPU:1, one launch (start us, length us, event | category | flops | bytes accessed | tf_op | source)
XLA Modules:
  0.0 519.2 jit_solution(354148787067696151)
XLA Ops:
  7.2 1.1 copy.69
  8.3 6.9 %collective-permute-start = (bf16[32,128]{1,0:T(8,128)(2,1)S(1)}, bf16[32,128]{1,0:T(8,128)(2,1)S(1)}, u32[]{:S(2)}, u32[]{:S(2)}) collective-permute-start(bf16[32,128]{1,0:T(8,128)(2,1)S(1)} %slice_bitcast_fusion), channel_id=1, source_target_pairs={{0,1},{1,2},{2,3},{3,4},{4,5},{5,6},{6,7},{7,8},{8,9},{9,10},{10,1... | collective-permute-start | bytes 24584 | tf_op jit(solution)/shard_map/ppermute | solution.py:16
  15.2 0.8 collective-permute-done
  18.6 0.7 copy-done.7
  19.3 1.3 fusion.62
  21.2 14.7 %all_to_all.21 = f32[16,1,64]{2,1,0:T(1,128)S(1)} all-to-all(f32[16,1,64]{2,1,0:T(1,128)S(1)} %broadcast_in_dim.15), channel_id=1, replica_groups=mesh['dp'=8,'sp_0'=4,'sp_1'=2,'sp_2'=2] {'sp_0','sp_1','sp_2'}, dimensions={0} | all-to-all | bytes 8192 | tf_op jit(solution)/shard_map/all_to_all | solution.py:21
  36.3 1.4 fusion.44
  37.8 0.7 all-gather.11.cloned.1.call-update
  39.4 3.1 fusion.65
  42.5 0.6 subtract_convert_fusion.2
  43.4 1.0 convolution_reduce_fusion
  44.4 1.3 convolution_subtract_fusion.1
  45.7 1.7 fusion.23
  47.5 33.8 %all-gather.7.cloned.1.call-done = bf16[16,128,256]{2,1,0:T(8,128)(2,1)} async-done(((bf16[16,8,256]{2,1,0:T(8,128)(2,1)}), bf16[16,128,256]{2,1,0:T(8,128)(2,1)}) %all-gather.7.cloned.1.call-update) | async-done | bytes 1048592 | tf_op jit(solution)/shard_map/all_gather | solution.py:151
  81.3 1.8 fusion.40
  83.1 1.8 multiply_reduce_fusion.1
  84.9 2.3 convolution_multiply_fusion
  87.2 86.0 %all-gather.11.cloned.1.call-done = bf16[1,2048,3072]{2,1,0:T(8,128)(2,1)} async-done(((bf16[1,128,3072]{2,1,0:T(8,128)(2,1)}), bf16[1,2048,3072]{2,1,0:T(8,128)(2,1)}) %all-gather.11.cloned.1.call-update) | async-done | bytes 12582928 | tf_op jit(solution)/shard_map/all_gather | solution.py:150
  173.2 12.1 %multiply_reduce_fusion = (f32[2048]{0:T(1024)S(1)}, bf16[2048,384]{0,1:T(8,128)(2,1)S(1)}, f32[384]{0:T(512)}) fusion(f32[2048,384]{0,1:T(8,128)} %convolution_multiply_fusion, f32[2048]{0:T(1024)S(1)} %add_rsqrt_fusion, f32[384]{0:T(512)} %convolution_reduce_fusion, bf16[1,2048,3072]{2,1,0:T(8,128)(2,1)} %all-gather.11.cloned.1.call-done, ...), kind=kOutput, calls=%fused_computation.18 | convolution fusion | flops 4855035392 | bytes 19692544 | tf_op jit(solution)/shard_map/dot_general | solution.py:117
  185.3 0.9 fusion.14
  186.2 1.0 copy.43
  187.3 9.0 %reduce-scatter.4.cloned.1.call-done = bf16[8,128,256]{2,1,0:T(8,128)(2,1)} async-done(((bf16[16,128,256]{2,1,0:T(8,128)(2,1)}), bf16[8,128,256]{2,1,0:T(8,128)(2,1)}) %reduce-scatter.4.cloned.1.call-update) | async-done | bytes 524304 | tf_op jit(solution)/shard_map/reduce_scatter | solution.py:48
  196.4 2.9 convolution_convert_fusion
  199.5 10.9 %multiply_convert_fusion = bf16[384,3072]{1,0:T(8,128)(2,1)S(1)} fusion(bf16[1,2048,3072]{2,1,0:T(8,128)(2,1)} %all-gather.11.cloned.1.call-done, f32[3072]{0:T(1024)S(1)} %copy-done.18, f32[2048,384]{0,1:T(8,128)} %convolution_multiply_fusion, f32[384]{0:T(512)S(1)} %copy-done.24), kind=kOutput, calls=%fused_computation.6 | convolution fusion | flops 4842061824 | bytes 18101760 | tf_op jit(solution)/shard_map/dot_general | solution.py:117
  210.5 1.7 copy.67
  212.1 5.0 reshape.113
  217.2 1.9 convert_subtract_fusion
  219.1 0.8 constant_dynamic-slice_fusion.1
  220.0 23.3 %all-gather.2 = f32[8,1,6528]{2,1,0:T(1,128)S(1)} all-gather(f32[1,1,6528]{2,1,0:T(1,128)S(1)} %reshape.119), channel_id=3, replica_groups=mesh['dp'=8,'sp_0'=4,'sp_1'=2,'sp_2'=2] {'dp'}, dimensions={0}, use_global_device_ids=true | all-gather | bytes 235008 | tf_op jit(solution)/shard_map/all_gather | solution.py:188
  243.2 26.6 %reduce-scatter.6.cloned.1.call-done = bf16[1,128,256]{2,1,0:T(8,128)(2,1)} async-done(((bf16[8,128,256]{2,1,0:T(8,128)(2,1)}), bf16[1,128,256]{2,1,0:T(8,128)(2,1)}) %reduce-scatter.6.cloned.1.call-update) | async-done | bytes 65552 | tf_op jit(solution)/shard_map/reduce_scatter | solution.py:49
  269.9 2.1 fusion.25
  272.6 1.0 reduce.10
  273.6 0.7 reshape.124
  274.3 7.2 %all-to-all-start.1 = ((bf16[16,2,1024]{2,1,0:T(2,128)(2,1)}), bf16[16,2,1024]{2,1,0:T(2,128)(2,1)S(1)}, u32[]{:S(2)}, u32[]{:S(2)}) async-start(bf16[16,2,1024]{2,1,0:T(2,128)(2,1)} %reshape.124), calls=%async_computation.3 | async-start | bytes 131072 | tf_op jit(solution)/shard_map/all_to_all | solution.py:198
  281.4 0.6 fusion.64
  282.1 7.1 %all-to-all-done.1 = bf16[16,2,1024]{2,1,0:T(2,128)(2,1)S(1)} async-done(((bf16[16,2,1024]{2,1,0:T(2,128)(2,1)}), bf16[16,2,1024]{2,1,0:T(2,128)(2,1)S(1)}, u32[]{:S(2)}, u32[]{:S(2)}) %all-to-all-start.1) | async-done | bytes 65568 | tf_op jit(solution)/shard_map/all_to_all | solution.py:198
  289.9 0.6 broadcast_in_dim.18
  290.5 3.7 all-to-all-start.2
  294.3 6.9 %all-to-all-done.2 = f32[16,1,64]{2,1,0:T(1,128)S(1)} async-done(((f32[16,1,64]{2,1,0:T(1,128)}), f32[16,1,64]{2,1,0:T(1,128)S(1)}, u32[]{:S(2)}, u32[]{:S(2)}) %all-to-all-start.2) | async-done | bytes 4128 | tf_op jit(solution)/shard_map/all_to_all | solution.py:21
  301.6 2.3 fusion.29
  304.0 1.5 multiply_convert_fusion.3
  305.5 1.4 fusion.45
  306.9 0.7 all-gather.9.cloned.1.call-done
  307.6 3.7 convolution_add_fusion.1
  311.3 41.8 %reduce-scatter.8.cloned.1.call-done = bf16[1152,128]{1,0:T(8,128)(2,1)} async-done(((bf16[9216,128]{1,0:T(8,128)(2,1)}), bf16[1152,128]{1,0:T(8,128)(2,1)}) %reduce-scatter.8.cloned.1.call-update) | async-done | bytes 294928 | tf_op jit(solution)/shard_map/reduce_scatter | solution.py:58
  353.1 1.9 reshape.116
  355.0 155.0 %all-reduce.3.cloned.1.call-done = f32[1152,256]{1,0:T(8,128)} async-done(((f32[1152,256]{1,0:T(8,128)}), f32[1152,256]{1,0:T(8,128)}) %all-reduce.3.cloned.1.call-update) | async-done | bytes 1179664 | tf_op jit(solution)/shard_map/psum | solution.py:220
  510.0 2.4 copy.81
  (122 shorter events, 6.2 us)
Async XLA Ops:
  7.2 36.3 %copy-start = (bf16[3072,384]{1,0:T(8,128)(2,1)S(1)}, bf16[3072,384]{1,0:T(8,128)(2,1)}, u32[]{:S(2)}) copy-start(bf16[3072,384]{1,0:T(8,128)(2,1)} %param.16) | copy-start | bytes 7077892
  7.2 74.1 %all-gather.7.cloned.1.call-start = ((), (), s32[]{:S(2)}) async-start(), calls=%async_computation.6 | async-start | bytes 1114112 | tf_op jit(solution)/shard_map/all_gather | solution.py:151
  8.3 7.7 %collective-permute-start = (bf16[32,128]{1,0:T(8,128)(2,1)S(1)}, bf16[32,128]{1,0:T(8,128)(2,1)S(1)}, u32[]{:S(2)}, u32[]{:S(2)}) collective-permute-start(bf16[32,128]{1,0:T(8,128)(2,1)S(1)} %slice_bitcast_fusion), channel_id=1, source_target_pairs={{0,1},{1,2},{2,3},{3,4},{4,5},{5,6},{6,7},{7,8},{8,9},{9,10},{10,1... | collective-permute-start | bytes 24584 | tf_op jit(solution)/shard_map/ppermute | solution.py:16
  18.6 0.7 copy-start.7
  36.2 7.2 %copy-start.14 = (f32[256]{0:T(256)}, f32[256]{0:T(256)S(1)}, u32[]{:S(2)}) copy-start(f32[256]{0:T(256)S(1)} %mul.219) | copy-start | bytes 3076
  36.3 7.1 %copy-start.16 = (f32[256]{0:T(256)}, f32[256]{0:T(256)S(1)}, u32[]{:S(2)}) copy-start(f32[256]{0:T(256)S(1)} %sub.53) | copy-start | bytes 3076
  37.7 135.5 %all-gather.11.cloned.1.call-start = ((), (), s32[]{:S(2)}) async-start(), calls=%async_computation.12 | async-start | bytes 13369344 | tf_op jit(solution)/shard_map/all_gather | solution.py:150
  38.5 157.8 %reduce-scatter.4.cloned.1.call-start = ((), (), s32[]{:S(2)}) async-start(), calls=%async_computation.7 | async-start | bytes 1572864 | tf_op jit(solution)/shard_map/reduce_scatter | solution.py:48
  38.5 4.6 copy-start.2
  43.1 2.7 copy-start.12
  43.4 4.1 copy-start.21
  81.2 1.8 copy-start.1
  81.3 1.8 copy-start.8
  83.1 1.9 copy-start.9
  173.2 12.1 %copy-start.3 = (f32[2048,256]{1,0:T(8,128)S(1)}, f32[2048,256]{1,0:T(8,128)}, u32[]{:S(2)}) copy-start(f32[2048,256]{1,0:T(8,128)} %get-tuple-element.24) | copy-start | bytes 6291460
  173.2 12.1 %copy-start.10 = (bf16[256,384]{1,0:T(8,128)(2,1)S(1)}, bf16[256,384]{1,0:T(8,128)(2,1)}, u32[]{:S(2)}) copy-start(bf16[256,384]{1,0:T(8,128)(2,1)} %fusion.23) | copy-start | bytes 589828
  185.3 2.0 copy-start.5
  186.2 13.3 %copy-start.18 = (f32[3072]{0:T(1024)S(1)}, f32[3072]{0:T(1024)}, u32[]{:S(2)}) copy-start(f32[3072]{0:T(1024)} %get-tuple-element.17) | copy-start | bytes 36868
  186.2 13.3 %copy-start.24 = (f32[384]{0:T(512)S(1)}, f32[384]{0:T(512)}, u32[]{:S(2)}) copy-start(f32[384]{0:T(512)} %convolution_reduce_fusion) | copy-start | bytes 4612
  187.3 82.6 %reduce-scatter.6.cloned.1.call-start = ((), (), s32[]{:S(2)}) async-start(), calls=%async_computation.8 | async-start | bytes 589824 | tf_op jit(solution)/shard_map/reduce_scatter | solution.py:49
  196.3 111.3 %all-gather.9.cloned.1.call-start = ((), (), s32[]{:S(2)}) async-start(), calls=%async_computation.10 | async-start | bytes 1769472 | tf_op jit(solution)/shard_map/all_gather | solution.py:187
  199.3 153.8 %reduce-scatter.8.cloned.1.call-start = ((), (), s32[]{:S(2)}) async-start(), calls=%async_computation.11 | async-start | bytes 2654208 | tf_op jit(solution)/shard_map/reduce_scatter | solution.py:58
  212.1 5.1 copy-start.22
  217.2 2.8 copy-start.11
  217.2 2.8 copy-start.13
  217.2 2.8 copy-start.23
  217.2 52.7 %copy-start.4 = (bf16[1,128,3072]{2,1,0:T(8,128)(2,1)S(1)}, bf16[1,128,3072]{2,1,0:T(8,128)(2,1)}, u32[]{:S(2)}) copy-start(bf16[1,128,3072]{2,1,0:T(8,128)(2,1)} %param.19) | copy-start | bytes 2359300
  219.1 70.1 %copy-start.15 = (f32[256]{0:T(256)S(1)}, f32[256]{0:T(256)}, u32[]{:S(2)}) copy-start(f32[256]{0:T(256)} %copy-done.14) | copy-start | bytes 3076
  219.1 70.1 %copy-start.17 = (f32[256]{0:T(256)S(1)}, f32[256]{0:T(256)}, u32[]{:S(2)}) copy-start(f32[256]{0:T(256)} %copy-done.16) | copy-start | bytes 3076
  219.1 70.1 %copy-start.19 = (f32[256]{0:T(256)S(1)}, f32[256]{0:T(256)}, u32[]{:S(2)}) copy-start(f32[256]{0:T(256)} %param.13) | copy-start | bytes 3076
  219.1 70.1 %copy-start.20 = (f32[256]{0:T(256)S(1)}, f32[256]{0:T(256)}, u32[]{:S(2)}) copy-start(f32[256]{0:T(256)} %param.12) | copy-start | bytes 3076
  272.0 32.0 %copy-start.6 = (f32[256,384]{1,0:T(8,128)S(1)}, f32[256,384]{1,0:T(8,128)}, u32[]{:S(2)}) copy-start(f32[256,384]{1,0:T(8,128)} %constant_dynamic-slice_fusion.1) | copy-start | bytes 1179652
  274.3 14.9 %all-to-all-start.1 = ((bf16[16,2,1024]{2,1,0:T(2,128)(2,1)}), bf16[16,2,1024]{2,1,0:T(2,128)(2,1)S(1)}, u32[]{:S(2)}, u32[]{:S(2)}) async-start(bf16[16,2,1024]{2,1,0:T(2,128)(2,1)} %reshape.124), calls=%async_computation.3 | async-start | bytes 131072 | tf_op jit(solution)/shard_map/all_to_all | solution.py:198
  290.5 10.7 %all-to-all-start.2 = ((f32[16,1,64]{2,1,0:T(1,128)}), f32[16,1,64]{2,1,0:T(1,128)S(1)}, u32[]{:S(2)}, u32[]{:S(2)}) async-start(f32[16,1,64]{2,1,0:T(1,128)} %broadcast_in_dim.18), calls=%async_computation.4 | async-start | bytes 16384 | tf_op jit(solution)/shard_map/all_to_all | solution.py:21
  294.2 215.8 %all-reduce.3.cloned.1.call-start = ((), (), s32[]{:S(2)}) async-start(), calls=%async_computation.9 | async-start | bytes 2359296 | tf_op jit(solution)/shard_map/psum | solution.py:220
Sparse Core Ops, SparseCore 0:
  37.8 43.3 all-gather.6
  83.6 89.5 all-gather.10
  187.4 8.8 reduce-scatter.3
  200.2 69.6 reduce-scatter.5
  271.4 36.1 all-gather.8
  309.9 43.1 reduce-scatter.7
  358.4 151.5 all-reduce.2
where the time goes:
time: 520 us; the launch traced here: 519 us
  waiting for transfers between devices  368 us (71%)
  matrix products  50.6 us (10%)
  blocking collectives  38 us (7%)
  local copies, waits for them, and re-layouts  20.8 us (4%)
  starting transfers between devices  18.2 us (4%)
  between operations  15.5 us (3%)
  other arithmetic  7.73 us (1%)
    psum x1, waiting for transfers between devices, on_device(): grad_conv = lax.psum(conv_local, DP_SP)  155 us
    all_gather x1, waiting for transfers between devices, on_device(): all_cot = lax.all_gather(cot_seq, SP, axis=0, tiled=True)  86 us
    reduce_scatter x1, waiting for transfers between devices, sum_packed(): lax.psum_scatter(lines, axis, tiled=True).reshape(-1)  41.8 us
    dot_general x8, matrix products, contract(): lax.dot_general(left, right, (((left_dim,), (right_dim,)), ((), ())), pre...  36.1 us
    all_gather x1, waiting for transfers between devices, on_device(): lax.all_gather(act_b.reshape(rows, cols, channel_count), SP, axis=1, tile...  33.8 us
    reduce_scatter x1, waiting for transfers between devices, sum_by_chip(): return lax.psum_scatter(parts, chips, scatter_dimension=0, tiled=True)[0]  26.6 us
    all_gather x1, blocking collectives, on_device(): lax.all_gather(jnp.concatenate([1.0 + scale, shift, dupper_sum]), 'dp', a...  23.3 us
    all_to_all x1, blocking collectives, copy_for_each(): lax.all_to_all(jnp.broadcast_to(array[None], (length, *array.shape)), axi...  14.7 us
  transfers between devices with their start and end apart: 10, of which 10 were waited for; matrix products, arithmetic and copies ran while one was open for 11% of the time, Pallas kernels for 0%

commit v1 on v0

--- a/solution.py
+++ b/solution.py
@@ -217,7 +217,7 @@
         )
     ).astype(jnp.bfloat16)
     conv_local = contract(patches, normed_gradient, 0, 0)
-    grad_conv = lax.psum(conv_local, DP_SP)
+    grad_conv = jnp.sum(lax.all_gather(conv_local, DP_SP), axis=0)
     return (grad_conv, grad_up, grad_down)
 
 

time: 520 us -> 1220 us (2.35)
  waiting for transfers between devices: 368 us -> 1020 us
  other arithmetic: 7.73 us -> 54.2 us
  blocking collectives: 38 us -> 62.2 us
    all_gather x0 -> x1, waiting for transfers between devices: none -> 815 us  [on_device(): grad_conv = jnp.sum(lax.all_gather(conv_local, DP_SP), axis=0)]
    psum x1 -> x0, waiting for transfers between devices: 155 us -> none  [on_device(): grad_conv = lax.psum(conv_local, DP_SP)]
    reduce_sum x0 -> x1, other arithmetic: none -> 46.5 us  [on_device(): grad_conv = jnp.sum(lax.all_gather(conv_local, DP_SP), axis=0)]
    reduce_scatter x1, waiting for transfers between devices: 26.6 us -> 52.7 us  [sum_by_chip(): return lax.psum_scatter(parts, chips, scatter_dimension=0, tiled=True)[0]]
    reduce_scatter x1, waiting for transfers between devices: 41.8 us -> 21.3 us  [sum_packed(): lax.psum_scatter(lines, axis, tiled=True).reshape(-1)]
    all_to_all x0 -> x1, blocking collectives: none -> 14.4 us  [on_device(): lax.all_to_all(dact.reshape(seq_rows, cols * devices_sp, channel_count).a...]
    all_to_all x2 -> x0, waiting for transfers between devices: 14 us -> none  [the longest x1 7.08 us: on_device(): lax.all_to_all(dact.reshape(seq_rows, cols * devices_sp, channel_count).a...]
    all_to_all x1 -> x2, blocking collectives: 14.7 us -> 24.6 us  [copy_for_each(): lax.all_to_all(jnp.broadcast_to(array[None], (length, *array.shape)), axi...]
  transfers between devices with their start and end apart: 10 -> 8, of which waited for: 10 -> 7; matrix products, arithmetic and copies ran while one was open for 11% -> 4% of each run, Pallas kernels for 0% -> 0%
where the time goes in v1:
time: 1220 us
  waiting for transfers between devices  1020 us (84%)
  blocking collectives  62.2 us (5%)
  other arithmetic  54.2 us (4%)
  matrix products  49.9 us (4%)
  local copies, waits for them, and re-layouts  15.8 us (1%)
  between operations  15.5 us (1%)
    all_gather x1, waiting for transfers between devices, on_device(): grad_conv = jnp.sum(lax.all_gather(conv_local, DP_SP), axis=0)  815 us
    all_gather x1, waiting for transfers between devices, on_device(): all_cot = lax.all_gather(cot_seq, SP, axis=0, tiled=True)  86 us
    reduce_scatter x1, waiting for transfers between devices, sum_by_chip(): return lax.psum_scatter(parts, chips, scatter_dimension=0, tiled=True)[0]  52.7 us
    reduce_sum x1, other arithmetic, on_device(): grad_conv = jnp.sum(lax.all_gather(conv_local, DP_SP), axis=0)  46.5 us
    dot_general x8, matrix products, contract(): lax.dot_general(left, right, (((left_dim,), (right_dim,)), ((), ())), pre...  36.1 us
    all_gather x1, waiting for transfers between devices, on_device(): lax.all_gather(act_b.reshape(rows, cols, channel_count), SP, axis=1, tile...  33.7 us
    all_to_all x2, blocking collectives, copy_for_each(): lax.all_to_all(jnp.broadcast_to(array[None], (length, *array.shape)), axi...  24.6 us
  transfers between devices with their start and end apart: 8, of which 7 were waited for; matrix products, arithmetic and copies ran while one was open for 4% of the time, Pallas kernels for 0%

profile of v1, /device:TPU:1, one launch (start us, length us, event | category | flops | bytes accessed | tf_op | source)
XLA Modules:
  0.0 1223.8 jit_solution(1751396892546272477)
XLA Ops:
  7.2 1.1 copy.69
  8.3 6.9 collective-permute-start
  15.2 0.8 collective-permute-done
  16.5 0.3 slice.64
  17.2 0.3 slice.67
  17.8 0.2 slice.69
  18.0 0.4 slice.70
  18.6 0.7 copy-done.6
  19.3 1.3 fusion.62
  21.2 14.7 %all_to_all.21 = f32[16,1,64]{2,1,0:T(1,128)S(1)} all-to-all(f32[16,1,64]{2,1,0:T(1,128)S(1)} %broadcast_in_dim.15), channel_id=1, replica_groups=mesh['dp'=8,'sp_0'=4,'sp_1'=2,'sp_2'=2] {'sp_0','sp_1','sp_2'}, dimensions={0} | all-to-all | bytes 8192 | tf_op jit(solution)/shard_map/all_to_all | solution.py:21
  36.3 1.4 fusion.44
  37.8 0.7 all-gather.13.cloned.1.call-update
  39.4 3.1 fusion.65
  42.5 0.6 subtract_convert_fusion.2
  43.1 0.3 convert_reduce_fusion
  43.4 1.0 convolution_reduce_fusion
  44.5 1.3 convolution_subtract_fusion.1
  45.8 1.7 fusion.23
  47.5 33.7 %all-gather.9.cloned.1.call-done = bf16[16,128,256]{2,1,0:T(8,128)(2,1)} async-done(((bf16[16,8,256]{2,1,0:T(8,128)(2,1)}), bf16[16,128,256]{2,1,0:T(8,128)(2,1)}) %all-gather.9.cloned.1.call-update) | async-done | bytes 1048592 | tf_op jit(solution)/shard_map/all_gather | solution.py:151
  81.3 1.8 fusion.40
  83.1 1.8 multiply_reduce_fusion.1
  84.9 2.3 convolution_multiply_fusion
  87.2 86.0 %all-gather.13.cloned.1.call-done = bf16[1,2048,3072]{2,1,0:T(8,128)(2,1)} async-done(((bf16[1,128,3072]{2,1,0:T(8,128)(2,1)}), bf16[1,2048,3072]{2,1,0:T(8,128)(2,1)}) %all-gather.13.cloned.1.call-update) | async-done | bytes 12582928 | tf_op jit(solution)/shard_map/all_gather | solution.py:150
  173.2 12.1 multiply_reduce_fusion
  185.3 0.9 fusion.14
  186.2 1.0 copy.43
  187.3 9.0 reduce-scatter.4.cloned.1.call-done
  196.4 2.8 convolution_convert_fusion
  199.3 0.2 reduce-scatter.8.cloned.1.call-start
  199.5 10.9 multiply_convert_fusion
  210.5 1.7 copy.67
  212.1 5.0 reshape.113
  217.3 52.7 %reduce-scatter.6.cloned.1.call-done = bf16[1,128,256]{2,1,0:T(8,128)(2,1)} async-done(((bf16[8,128,256]{2,1,0:T(8,128)(2,1)}), bf16[1,128,256]{2,1,0:T(8,128)(2,1)}) %reduce-scatter.6.cloned.1.call-update) | async-done | bytes 65552 | tf_op jit(solution)/shard_map/reduce_scatter | solution.py:49
  269.9 2.1 fusion.25
  272.1 0.5 broadcast.121
  272.6 1.0 reduce.10
  273.7 14.4 %all_to_all.22 = bf16[16,2,1024]{2,1,0:T(2,128)(2,1)S(1)} all-to-all(bf16[16,2,1024]{2,1,0:T(2,128)(2,1)S(1)} %reshape.125), channel_id=1, replica_groups=mesh['dp'=8,'sp_0'=4,'sp_1'=2,'sp_2'=2] {'sp_0','sp_1','sp_2'}, dimensions={0} | all-to-all | bytes 131072 | tf_op jit(solution)/shard_map/all_to_all | solution.py:198
  288.8 9.9 all_to_all.23
  299.1 2.3 fusion.29
  301.5 1.8 convert_subtract_fusion
  303.4 23.2 %all-gather.3 = f32[8,1,6528]{2,1,0:T(1,128)S(1)} all-gather(f32[1,1,6528]{2,1,0:T(1,128)S(1)} %reshape.120), channel_id=4, replica_groups=mesh['dp'=8,'sp_0'=4,'sp_1'=2,'sp_2'=2] {'dp'}, dimensions={0}, use_global_device_ids=true | all-gather | bytes 235008 | tf_op jit(solution)/shard_map/all_gather | solution.py:188
  326.7 0.7 fusion.45
  327.4 1.5 multiply_convert_fusion.3
  328.9 3.7 convolution_add_fusion.1
  332.6 21.3 %reduce-scatter.8.cloned.1.call-done = bf16[1152,128]{1,0:T(8,128)(2,1)} async-done(((bf16[9216,128]{1,0:T(8,128)(2,1)}), bf16[1152,128]{1,0:T(8,128)(2,1)}) %reduce-scatter.8.cloned.1.call-update) | async-done | bytes 294928 | tf_op jit(solution)/shard_map/reduce_scatter | solution.py:58
  353.9 1.9 reshape.116
  355.8 814.5 %all-gather.15.cloned.1.call-done = f32[147456,256]{1,0:T(8,128)} async-done(((f32[1152,256]{1,0:T(8,128)}), f32[147456,256]{1,0:T(8,128)}) %all-gather.15.cloned.1.call-update) | async-done | bytes 150994960 | tf_op jit(solution)/shard_map/all_gather | solution.py:220
  1170.4 46.5 %reduce_sum.154 = f32[1152,256]{1,0:T(8,128)} reduce(f32[128,1152,256]{2,1,0:T(8,128)} %bitcast.19, f32[]{:T(128)} %constant.18.clone.1), dimensions={0}, to_apply=%region_16.17 | reduce | flops 37453824 | bytes 152174592 | tf_op jit(solution)/shard_map/reduce_sum | solution.py:220
  (118 shorter events, 4.0 us)
Async XLA Ops:
  7.2 36.3 %copy-start = (bf16[3072,384]{1,0:T(8,128)(2,1)S(1)}, bf16[3072,384]{1,0:T(8,128)(2,1)}, u32[]{:S(2)}) copy-start(bf16[3072,384]{1,0:T(8,128)(2,1)} %param.16) | copy-start | bytes 7077892
  7.2 74.1 %all-gather.9.cloned.1.call-start = ((), (), s32[]{:S(2)}) async-start(), calls=%async_computation.6 | async-start | bytes 1114112 | tf_op jit(solution)/shard_map/all_gather | solution.py:151
  8.3 7.7 collective-permute-start
  18.6 0.7 copy-start.6
  36.2 7.2 copy-start.13
  36.3 7.1 copy-start.15
  37.7 135.5 %all-gather.13.cloned.1.call-start = ((), (), s32[]{:S(2)}) async-start(), calls=%async_computation.11 | async-start | bytes 13369344 | tf_op jit(solution)/shard_map/all_gather | solution.py:150
  38.5 157.9 %reduce-scatter.4.cloned.1.call-start = ((), (), s32[]{:S(2)}) async-start(), calls=%async_computation.7 | async-start | bytes 1572864 | tf_op jit(solution)/shard_map/reduce_scatter | solution.py:48
  38.5 4.6 copy-start.2
  43.1 2.7 copy-start.11
  43.4 4.1 copy-start.20
  81.2 1.8 copy-start.1
  81.3 1.8 copy-start.7
  83.1 1.9 copy-start.8
  173.2 12.1 copy-start.3
  173.2 12.1 copy-start.9
  185.3 2.0 copy-start.5
  186.2 13.3 %copy-start.17 = (f32[3072]{0:T(1024)S(1)}, f32[3072]{0:T(1024)}, u32[]{:S(2)}) copy-start(f32[3072]{0:T(1024)} %get-tuple-element.17) | copy-start | bytes 36868
  186.2 13.3 %copy-start.23 = (f32[384]{0:T(512)S(1)}, f32[384]{0:T(512)}, u32[]{:S(2)}) copy-start(f32[384]{0:T(512)} %convolution_reduce_fusion) | copy-start | bytes 4612
  187.3 82.7 %reduce-scatter.6.cloned.1.call-start = ((), (), s32[]{:S(2)}) async-start(), calls=%async_computation.8 | async-start | bytes 589824 | tf_op jit(solution)/shard_map/reduce_scatter | solution.py:49
  196.4 132.5 %all-gather.11.cloned.1.call-start = ((), (), s32[]{:S(2)}) async-start(), calls=%async_computation.9 | async-start | bytes 1769472 | tf_op jit(solution)/shard_map/all_gather | solution.py:187
  199.3 154.7 %reduce-scatter.8.cloned.1.call-start = ((), (), s32[]{:S(2)}) async-start(), calls=%async_computation.10 | async-start | bytes 2654208 | tf_op jit(solution)/shard_map/reduce_scatter | solution.py:58
  212.1 57.8 %copy-start.4 = (bf16[1,128,3072]{2,1,0:T(8,128)(2,1)S(1)}, bf16[1,128,3072]{2,1,0:T(8,128)(2,1)}, u32[]{:S(2)}) copy-start(bf16[1,128,3072]{2,1,0:T(8,128)(2,1)} %param.19) | copy-start | bytes 2359300
  217.2 71.0 %copy-start.14 = (f32[256]{0:T(256)S(1)}, f32[256]{0:T(256)}, u32[]{:S(2)}) copy-start(f32[256]{0:T(256)} %copy-done.13) | copy-start | bytes 3076
  217.2 71.0 %copy-start.16 = (f32[256]{0:T(256)S(1)}, f32[256]{0:T(256)}, u32[]{:S(2)}) copy-start(f32[256]{0:T(256)} %copy-done.15) | copy-start | bytes 3076
  217.2 71.0 %copy-start.18 = (f32[256]{0:T(256)S(1)}, f32[256]{0:T(256)}, u32[]{:S(2)}) copy-start(f32[256]{0:T(256)} %param.13) | copy-start | bytes 3076
  217.2 71.0 %copy-start.19 = (f32[256]{0:T(256)S(1)}, f32[256]{0:T(256)}, u32[]{:S(2)}) copy-start(f32[256]{0:T(256)} %param.12) | copy-start | bytes 3076
  217.2 84.3 %copy-start.21 = (f32[256]{0:T(256)S(1)}, f32[256]{0:T(256)}, u32[]{:S(2)}) copy-start(f32[256]{0:T(256)} %copy-done.20) | copy-start | bytes 3076
  217.2 953.2 %all-gather.15.cloned.1.call-start = ((), (), s32[]{:S(2)}) async-start(), calls=%async_computation.12 | async-start | bytes 152174592 | tf_op jit(solution)/shard_map/all_gather | solution.py:220
  301.5 1.9 copy-start.10
  301.5 1.9 copy-start.12
  301.5 1.9 copy-start.22
Sparse Core Ops, SparseCore 0:
  37.8 43.3 all-gather.8
  83.6 89.5 all-gather.12
  187.4 8.8 reduce-scatter.3
  200.2 69.7 reduce-scatter.5
  272.0 36.1 all-gather.10
  310.5 43.4 reduce-scatter.7
  356.2 814.0 all-gather.14
